TPU v7x, 32 devices: a whole 2x2x4 slice. The times are simulated.
32 devices in a mesh: lat: 8 (over z, core), lon: 4 (over y, x).
Axes of the slice: x: 2, y: 2, z: 4, core: 2. Of those that a mesh axis runs over, the one named last changes fastest.
Arguments:
- predicted_state: float32 [1440, 13312], P('lon', 'lat'), may hold values from -24 to 24
- verified_state: float32 [1440, 13312], P('lon', 'lat'), may hold values from -20 to 20
- normal_state: float32 [1440, 13312], P('lon', 'lat'), may hold values from -3 to 3
Outputs:
- energy_curves: float32 [3, 52, 721], replicated
- rms_error: float32 [52], replicated
- anomaly_corr: float32 [52], replicated
All inputs are finite; a program needn't handle non-finite values.
Results may differ from a plain program's by a relative error of at most 0.00005.
Values sent between devices are 32-bit elements; how exact they have to be, the bound alone decides.
A program may use at most 64 MiB of HBM per device.

v0:
```python
import jax
import jax.numpy as jnp
from jax import lax
from jax.sharding import PartitionSpec as P

FIELDS = 52
epsilon = 1e-06


def latitude_weights(lat_index, parallel_number):
    return jnp.cos(jnp.pi * ((lat_index.astype(jnp.float32) + 0.5) / parallel_number - 0.5))


def dft_table(lon_rows, lon_total, wave_count):
    longitudes = jnp.arange(lon_rows, dtype=jnp.int32)
    waves = jnp.arange(wave_count, dtype=jnp.int32)
    phase = longitudes[:, None] * waves[None, :] % lon_total
    angle = 2.0 * jnp.pi / lon_total * phase.astype(jnp.float32)
    return jnp.concatenate([jnp.cos(angle), -jnp.sin(angle)], axis=1)


def transform_columns(stacked, table):
    return lax.dot_general(
        stacked,
        table,
        (((0,), (0,)), ((), ())),
        precision=lax.Precision.HIGHEST,
        preferred_element_type=jnp.float32,
    )


def row_powers(fore_coeffs, true_coeffs, wave_count):
    diff_coeffs = fore_coeffs - true_coeffs

    def square(coeffs):
        return (
            coeffs[:, :wave_count] * coeffs[:, :wave_count]
            + coeffs[:, wave_count:] * coeffs[:, wave_count:]
        )

    return jnp.stack([square(fore_coeffs), square(true_coeffs), square(diff_coeffs)], axis=1)


def local(predicted_state, verified_state, normal_state):
    quantity_labels = FIELDS
    meridian_lines, meridian_number = predicted_state.shape
    parallel_lines = meridian_number // quantity_labels
    parallel_number = parallel_lines * lax.axis_size("lat")
    lon_devices = lax.axis_size("lon")
    lon_total = meridian_lines * lon_devices
    wave_count = lon_total // 2 + 1
    row_share = meridian_number // lon_devices
    lat_first = lax.axis_index("lat") * parallel_lines
    weights = latitude_weights(
        lat_first + jnp.arange(parallel_lines, dtype=jnp.int32), parallel_number
    )
    weight_total = jnp.sum(
        latitude_weights(jnp.arange(parallel_number, dtype=jnp.int32), parallel_number)
    )
    predicted_block = predicted_state.reshape(meridian_lines, parallel_lines, quantity_labels)
    observed_block = verified_state.reshape(meridian_lines, parallel_lines, quantity_labels)
    normal_block = normal_state.reshape(meridian_lines, parallel_lines, quantity_labels)
    mismatch_parts = predicted_block - observed_block
    predicted_anomalies = predicted_block - normal_block
    observed_anomalies = observed_block - normal_block
    broad_layout = weights[None, :, None]
    skill_terms = jnp.stack(
        [
            jnp.sum(broad_layout * mismatch_parts * mismatch_parts, axis=(0, 1)),
            jnp.sum(broad_layout * predicted_anomalies * observed_anomalies, axis=(0, 1)),
            jnp.sum(broad_layout * predicted_anomalies * predicted_anomalies, axis=(0, 1)),
            jnp.sum(broad_layout * observed_anomalies * observed_anomalies, axis=(0, 1)),
        ]
    )
    predicted_meridians = predicted_block.transpose(0, 2, 1).reshape(
        meridian_lines, meridian_number
    )
    true_cols = observed_block.transpose(0, 2, 1).reshape(meridian_lines, meridian_number)
    full_table = dft_table(lon_total, lon_total, wave_count)
    fore_blocks = predicted_meridians.reshape(meridian_lines, lon_devices, row_share)
    true_blocks = true_cols.reshape(meridian_lines, lon_devices, row_share)
    fore_part = lax.all_to_all(fore_blocks, "lon", split_axis=1, concat_axis=0, tiled=True)[:, 0, :]
    true_part = lax.all_to_all(true_blocks, "lon", split_axis=1, concat_axis=0, tiled=True)[:, 0, :]
    items = fore_part.shape[1]
    stacked = jnp.concatenate([fore_part, true_part], axis=1)
    coeffs = transform_columns(stacked, full_table)
    powers = row_powers(coeffs[:items], coeffs[items:], wave_count)
    share_start = lax.axis_index("lon") * row_share
    global_cols = share_start + jnp.arange(row_share, dtype=jnp.int32)
    field_of = global_cols // parallel_lines
    row_weights = latitude_weights(lat_first + global_cols % parallel_lines, parallel_number)
    row_scale = row_weights / (lon_total * lon_total * weight_total)
    weighted = powers.reshape(row_share, 3 * wave_count) * row_scale[:, None]
    field_index = jnp.arange(quantity_labels, dtype=jnp.int32)
    window = min(quantity_labels, row_share // parallel_lines + 2)
    first_field = share_start // parallel_lines
    window_index = jnp.arange(window, dtype=jnp.int32)
    offset = field_of - first_field
    selector = (offset[None, :] == window_index[:, None]).astype(jnp.float32)
    band_sum = jnp.dot(
        selector, weighted, precision=lax.Precision.HIGHEST, preferred_element_type=jnp.float32
    )
    band_sum = lax.psum(band_sum, "lat")
    gathered = lax.all_gather(band_sum, "lon", axis=0, tiled=True)
    slot_index = jnp.arange(lon_devices * window, dtype=jnp.int32)
    slot_field = slot_index // window * row_share // parallel_lines + slot_index % window
    placer = (slot_field[None, :] == field_index[:, None]).astype(jnp.float32)
    summed = jnp.dot(
        placer, gathered, precision=lax.Precision.HIGHEST, preferred_element_type=jnp.float32
    )
    energy_curves = summed.reshape(quantity_labels, 3, wave_count).transpose(1, 0, 2)
    skill_means = lax.psum(skill_terms, ("lat", "lon")) / (lon_total * weight_total)
    rms_error = jnp.sqrt(skill_means[0])
    anomaly_corr = skill_means[1] / jnp.sqrt(
        (skill_means[2] + epsilon) * (skill_means[3] + epsilon)
    )
    return (energy_curves, rms_error, anomaly_corr)


def solution(mesh):
    in_specs = (P("lon", "lat"), P("lon", "lat"), P("lon", "lat"))
    out_specs = (P(), P(), P())
    return jax.shard_map(local, mesh=mesh, in_specs=in_specs, out_specs=out_specs, check_vma=False)
```

profile of v0, /device:TPU:8, one launch (start us, length us, event | category | flops | bytes accessed | tf_op | source)
XLA Modules:
  0.0 275.4 jit_solution(18060614692774121550)
XLA Ops:
  7.2 3.2 %copy.26 = f32[360,1664]{0,1:T(8,128)} copy(f32[360,1664]{1,0:T(8,128)} %param.4) | data formatting | bytes 4792320 | tf_op args[1]
  10.4 2.4 reshape.125
  12.8 1.9 copy.27
  14.8 0.0 copy-start
  14.8 4.8 %all-to-all-start.1 = ((f32[360,4,416]{0,2,1:T(8,128)}), f32[360,4,416]{0,2,1:T(8,128)}, u32[]{:S(2)}, u32[]{:S(2)}) async-start(f32[360,4,416]{0,2,1:T(8,128)} %bitcast.41), calls=%async_computation.1 | async-start | bytes 5111808 | tf_op jit(solution)/shard_map/all_to_all | solution.py:83
  19.5 0.0 copy-done
  19.6 2.2 copy.23
  21.7 2.4 reshape.124
  24.2 2.1 copy.24
  26.3 0.1 mul.170
  26.4 0.1 mul.171
  26.5 23.2 %all-to-all-done.1 = f32[360,4,416]{0,2,1:T(8,128)} async-done(((f32[360,4,416]{0,2,1:T(8,128)}), f32[360,4,416]{0,2,1:T(8,128)}, u32[]{:S(2)}, u32[]{:S(2)}) %all-to-all-start.1) | async-done | bytes 2396192 | tf_op jit(solution)/shard_map/all_to_all | solution.py:83
  49.7 3.6 %all-to-all-start = ((f32[360,4,416]{0,2,1:T(8,128)}), f32[360,4,416]{0,2,1:T(8,128)S(1)}, u32[]{:S(2)}, u32[]{:S(2)}) async-start(f32[360,4,416]{0,2,1:T(8,128)} %bitcast.39), calls=%async_computation | async-start | bytes 5111808 | tf_op jit(solution)/shard_map/all_to_all | solution.py:82
  53.3 0.0 all-reduce.2.cloned.1.call-start
  53.4 4.3 %fusion.17 = (f32[1664]{0:T(1024)S(1)}, f32[1664]{0:T(1024)S(1)}, f32[1664]{0:T(1024)S(1)}, f32[1664]{0:T(1024)S(1)}) fusion(f32[360,1664]{1,0:T(8,128)} %param.3, f32[360,1664]{1,0:T(8,128)} %param.4, f32[1664]{0:T(1024)S(1)} %mul.171, f32[360,1664]{1,0:T(8,128)} %param.5), kind=kLoop, calls=%fused_computation.26 | loop fusion | flops 8379904 | bytes 7221760 | tf_op jit(solution)/shard_map/reduce_sum | solution.py:69
  57.6 0.1 reduce_sum.84
  57.7 0.1 reduce_sum.81
  57.9 0.1 reduce_sum.62
  58.0 0.1 reduce_sum.59
  58.1 0.7 cosine_reduce_fusion
  60.1 55.8 %psum.15 = f32[4,52]{1,0:T(4,128)S(1)} all-reduce(f32[4,52]{1,0:T(4,128)S(1)} %pad_maximum_fusion.1), channel_id=1, replica_groups=mesh['lat'=8,'lon'=4] {'lat','lon'}, use_global_device_ids=true, to_apply=%region_10.11 | all-reduce | flops 208 | bytes 1664 | tf_op jit(solution)/shard_map/psum | solution.py:112
  115.9 0.1 fusion.37
  116.0 0.5 multiply_bitcast_fusion
  116.5 19.7 %sine_negate_fusion = (f32[1440,721]{1,0:T(8,128)}, f32[1440,721]{1,0:T(8,128)}) fusion(), kind=kLoop, calls=%fused_computation.12 | loop fusion | flops 10382400 | bytes 8305920 | tf_op jit(solution)/shard_map/neg | solution.py:19
  136.2 4.8 %copy.28 = f32[4,360,1,416]{1,0,3,2:T(4,128)} copy(f32[4,360,1,416]{1,3,0,2:T(8,128)} %bitcast.7) | data formatting | bytes 4792320 | tf_op jit(solution)/shard_map/all_to_all | solution.py:83
  141.1 4.0 %squeeze.5 = f32[1440,416]{0,1:T(8,128)} reshape(f32[4,360,1,416]{1,0,3,2:T(4,128)} %copy.28) | data formatting | bytes 4792320 | tf_op jit(solution)/shard_map/squeeze | solution.py:83
  145.1 0.0 all-to-all-done
  145.1 3.1 %copy.25 = f32[4,360,1,416]{1,0,3,2:T(4,128)} copy(f32[4,360,1,416]{1,3,0,2:T(8,128)S(1)} %bitcast.40) | data formatting | bytes 4792320 | tf_op jit(solution)/shard_map/all_to_all | solution.py:82
  148.2 0.0 copy-start.1
  148.2 4.2 %squeeze.4 = f32[1440,416]{0,1:T(8,128)} reshape(f32[4,360,1,416]{1,0,3,2:T(4,128)} %copy.25) | data formatting | bytes 4792320 | tf_op jit(solution)/shard_map/squeeze | solution.py:82
  152.4 0.0 copy-done.1
  152.4 29.4 %fusion = f32[832,1442]{1,0:T(8,128)S(1)} fusion(f32[1440,721]{1,0:T(8,128)} %get-tuple-element.20, f32[1440,721]{1,0:T(8,128)} %get-tuple-element.21, f32[1440,416]{0,1:T(8,128)S(1)} %copy-done.1, f32[1440,416]{0,1:T(8,128)} %squeeze.4), kind=kOutput, calls=%fused_computation | convolution fusion | flops 20734851072 | bytes 17897216 | tf_op jit(solution)/shard_map/dot_general | solution.py:23
  181.9 0.4 slice_subtract_fusion
  182.3 0.7 fusion.25
  183.0 0.4 fusion.21
  183.4 2.1 pad_maximum_fusion
  185.5 5.6 %copy.29 = f32[416,3,721]{0,2,1:T(8,128)} copy(f32[416,3,721]{2,0,1:T(8,128)} %pad_maximum_fusion) | data formatting | bytes 7198464 | tf_op jit(solution)/shard_map/stack | solution.py:41
  191.1 4.9 %reshape.126 = f32[416,2163]{0,1:T(8,128)} reshape(f32[416,3,721]{0,2,1:T(8,128)} %copy.29) | data formatting | bytes 7198464 | tf_op jit(solution)/shard_map/reshape | solution.py:93
  196.0 5.2 %fusion.7 = f32[15,2163]{1,0:T(8,128)} fusion(f32[416,2163]{0,1:T(8,128)} %reshape.126, f32[416]{0:T(512)S(1)} %fusion.37, s32[416]{0:T(512)S(1)} %fusion.29), kind=kOutput, calls=%fused_computation.8 | convolution fusion | flops 162871488 | bytes 3732340 | tf_op jit(solution)/shard_map/dot_general | solution.py:100
  201.2 0.0 all-reduce.2.cloned.1.call-update
  201.2 54.4 %all-reduce.2.cloned.1.call-done = f32[15,2163]{1,0:T(8,128)} async-done(((f32[15,2163]{1,0:T(8,128)}), f32[15,2163]{1,0:T(8,128)}) %all-reduce.2.cloned.1.call-update) | async-done | bytes 129796 | tf_op jit(solution)/shard_map/psum | solution.py:103
  255.6 11.1 %all-gather = f32[4,15,2163]{2,1,0:T(8,128)S(1)} all-gather(f32[1,15,2163]{2,1,0:T(8,128)} %bitcast.43), channel_id=1, replica_groups=mesh['lat'=8,'lon'=4] {'lon'}, dimensions={0}, use_global_device_ids=true | all-gather | bytes 648900 | tf_op jit(solution)/shard_map/all_gather | solution.py:104
  266.7 0.1 reshape.129
  266.8 0.4 fusion.26
  267.2 0.4 reshape.127
  267.7 0.9 copy.30
  (9 shorter events, 0.2 us)
Async XLA Ops:
  14.8 4.8 %copy-start = (f32[360,1664]{1,0:T(8,128)S(1)}, f32[360,1664]{1,0:T(8,128)}, u32[]{:S(2)}) copy-start(f32[360,1664]{1,0:T(8,128)} %param.3) | copy-start | bytes 7188484
  14.8 34.9 %all-to-all-start.1 = ((f32[360,4,416]{0,2,1:T(8,128)}), f32[360,4,416]{0,2,1:T(8,128)}, u32[]{:S(2)}, u32[]{:S(2)}) async-start(f32[360,4,416]{0,2,1:T(8,128)} %bitcast.41), calls=%async_computation.1 | async-start | bytes 5111808 | tf_op jit(solution)/shard_map/all_to_all | solution.py:83
  49.7 95.4 %all-to-all-start = ((f32[360,4,416]{0,2,1:T(8,128)}), f32[360,4,416]{0,2,1:T(8,128)S(1)}, u32[]{:S(2)}, u32[]{:S(2)}) async-start(f32[360,4,416]{0,2,1:T(8,128)} %bitcast.39), calls=%async_computation | async-start | bytes 5111808 | tf_op jit(solution)/shard_map/all_to_all | solution.py:82
  53.3 202.3 %all-reduce.2.cloned.1.call-start = ((), (), s32[]{:S(2)}) async-start(), calls=%async_computation.2 | async-start | bytes 278528 | tf_op jit(solution)/shard_map/psum | solution.py:103
  148.2 4.2 %copy-start.1 = (f32[1440,416]{0,1:T(8,128)S(1)}, f32[1440,416]{0,1:T(8,128)}, u32[]{:S(2)}) copy-start(f32[1440,416]{0,1:T(8,128)} %squeeze.5) | copy-start | bytes 7188484
Sparse Core Ops, SparseCore 0:
  201.3 54.3 all-reduce.1
where the time goes:
time: 276 us; the launch traced here: 275 us
  waiting for transfers between devices  77.7 us (28%)
  blocking collectives  66.9 us (24%)
  local copies, waits for them, and re-layouts  42.9 us (16%)
  matrix products  35 us (13%)
  other arithmetic  29 us (11%)
  between operations  15.5 us (6%)
  starting transfers between devices  8.44 us (3%)
    psum x1, blocking collectives, local(): lax.psum(skill_terms, ('lat', 'lon')) / (lon_total * weight_total)  55.8 us
    psum x1, waiting for transfers between devices, local(): band_sum = lax.psum(band_sum, 'lat')  54.4 us
    dot_general x1, matrix products, transform_columns(): lax.dot_general(stacked, table, (((0,), (0,)), ((), ())), precision=lax.P...  29.4 us
    all_to_all x1, waiting for transfers between devices, local(): lax.all_to_all(true_blocks, 'lon', split_axis=1, concat_axis=0, tiled=True)  23.2 us
    neg x1, other arithmetic, dft_table(): return jnp.concatenate([jnp.cos(angle), -jnp.sin(angle)], axis=1)  19.7 us
    all_gather x1, blocking collectives, local(): gathered = lax.all_gather(band_sum, 'lon', axis=0, tiled=True)  11.1 us
    unnamed x8, local copies, waits for them, and re-layouts  6.34 us
    another operation x1, local copies, waits for them, and re-layouts, row_powers(): jnp.stack([square(fore_coeffs), square(true_coeffs), square(diff_coeffs)]...  5.61 us
  transfers between devices with their start and end apart: 3, of which 2 were waited for; matrix products, arithmetic and copies ran while one was open for 15% of the time, Pallas kernels for 0%

commit v1 on v0

--- a/solution.py
+++ b/solution.py
@@ -109,7 +109,9 @@
         placer, gathered, precision=lax.Precision.HIGHEST, preferred_element_type=jnp.float32
     )
     energy_curves = summed.reshape(quantity_labels, 3, wave_count).transpose(1, 0, 2)
-    skill_means = lax.psum(skill_terms, ("lat", "lon")) / (lon_total * weight_total)
+    skill_means = jnp.sum(lax.all_gather(skill_terms, ("lat", "lon")), axis=0) / (
+        lon_total * weight_total
+    )
     rms_error = jnp.sqrt(skill_means[0])
     anomaly_corr = skill_means[1] / jnp.sqrt(
         (skill_means[2] + epsilon) * (skill_means[3] + epsilon)

time: 276 us -> 299 us (1.083)
  blocking collectives: 66.9 us -> 81.8 us
  waiting for transfers between devices: 77.7 us -> 85.7 us
    all_gather x0 -> x1, blocking collectives: none -> 70.7 us  [local(): lax.all_gather(skill_terms, ('lat', 'lon'))]
    psum x1 -> x0, blocking collectives: 55.8 us -> none  [local(): lax.psum(skill_terms, ('lat', 'lon')) / (lon_total * weight_total)]
    psum x1, waiting for transfers between devices: 54.4 us -> 62.5 us  [local(): band_sum = lax.psum(band_sum, 'lat')]
  transfers between devices with their start and end apart: 3 -> 3, of which waited for: 2 -> 2; matrix products, arithmetic and copies ran while one was open for 15% -> 14% of each run, Pallas kernels for 0% -> 0%
where the time goes in v1:
time: 299 us; the launch traced here: 298 us
  waiting for transfers between devices  85.7 us (29%)
  blocking collectives  81.8 us (27%)
  local copies, waits for them, and re-layouts  42.9 us (14%)
  matrix products  35 us (12%)
  other arithmetic  29.1 us (10%)
  between operations  15.5 us (5%)
  starting transfers between devices  8.44 us (3%)
    all_gather x1, blocking collectives, local(): lax.all_gather(skill_terms, ('lat', 'lon'))  70.7 us
    psum x1, waiting for transfers between devices, local(): band_sum = lax.psum(band_sum, 'lat')  62.5 us
    dot_general x1, matrix products, transform_columns(): lax.dot_general(stacked, table, (((0,), (0,)), ((), ())), precision=lax.P...  29.4 us
    all_to_all x1, waiting for transfers between devices, local(): lax.all_to_all(true_blocks, 'lon', split_axis=1, concat_axis=0, tiled=True)  23.2 us
    neg x1, other arithmetic, dft_table(): return jnp.concatenate([jnp.cos(angle), -jnp.sin(angle)], axis=1)  19.7 us
    all_gather x1, blocking collectives, local(): gathered = lax.all_gather(band_sum, 'lon', axis=0, tiled=True)  11.1 us
    unnamed x8, local copies, waits for them, and re-layouts  6.34 us
  transfers between devices with their start and end apart: 3, of which 2 were waited for; matrix products, arithmetic and copies ran while one was open for 14% of the time, Pallas kernels for 0%

profile of v1, /device:TPU:8, one launch (start us, length us, event | category | flops | bytes accessed | tf_op | source)
XLA Modules:
  0.0 298.4 jit_solution(9999908452201834138)
XLA Ops:
  7.2 3.2 %copy.26 = f32[360,1664]{0,1:T(8,128)} copy(f32[360,1664]{1,0:T(8,128)} %param.4) | data formatting | bytes 4792320 | tf_op args[1]
  10.4 2.4 reshape.125
  12.8 1.9 copy.27
  14.8 0.0 copy-start
  14.8 4.8 %all-to-all-start.1 = ((f32[360,4,416]{0,2,1:T(8,128)}), f32[360,4,416]{0,2,1:T(8,128)}, u32[]{:S(2)}, u32[]{:S(2)}) async-start(f32[360,4,416]{0,2,1:T(8,128)} %bitcast.43), calls=%async_computation.1 | async-start | bytes 5111808 | tf_op jit(solution)/shard_map/all_to_all | solution.py:83
  19.5 0.0 copy-done
  19.6 2.2 copy.23
  21.7 2.4 reshape.124
  24.2 2.1 copy.24
  26.3 0.1 mul.170
  26.4 0.1 mul.171
  26.5 23.2 %all-to-all-done.1 = f32[360,4,416]{0,2,1:T(8,128)} async-done(((f32[360,4,416]{0,2,1:T(8,128)}), f32[360,4,416]{0,2,1:T(8,128)}, u32[]{:S(2)}, u32[]{:S(2)}) %all-to-all-start.1) | async-done | bytes 2396192 | tf_op jit(solution)/shard_map/all_to_all | solution.py:83
  49.7 3.6 %all-to-all-start = ((f32[360,4,416]{0,2,1:T(8,128)}), f32[360,4,416]{0,2,1:T(8,128)S(1)}, u32[]{:S(2)}, u32[]{:S(2)}) async-start(f32[360,4,416]{0,2,1:T(8,128)} %bitcast.41), calls=%async_computation | async-start | bytes 5111808 | tf_op jit(solution)/shard_map/all_to_all | solution.py:82
  53.3 0.0 all-reduce.2.cloned.1.call-start
  53.4 4.3 %fusion.17 = (f32[1664]{0:T(1024)S(1)}, f32[1664]{0:T(1024)S(1)}, f32[1664]{0:T(1024)S(1)}, f32[1664]{0:T(1024)S(1)}) fusion(f32[360,1664]{1,0:T(8,128)} %param.3, f32[360,1664]{1,0:T(8,128)} %param.4, f32[1664]{0:T(1024)S(1)} %mul.171, f32[360,1664]{1,0:T(8,128)} %param.5), kind=kLoop, calls=%fused_computation.26 | loop fusion | flops 8379904 | bytes 7221760 | tf_op jit(solution)/shard_map/reduce_sum | solution.py:69
  57.6 0.1 reduce_sum.93
  57.7 0.1 reduce_sum.90
  57.9 0.1 reduce_sum.73
  58.0 0.1 reduce_sum.67
  58.1 70.7 %all-gather.2 = f32[32,4,52]{2,1,0:T(4,128)S(1)} all-gather(f32[1,4,52]{2,1,0:T(4,128)S(1)} %maximum_bitcast_fusion), channel_id=2, replica_groups=mesh['lat'=8,'lon'=4] {'lat','lon'}, dimensions={0}, use_global_device_ids=true | all-gather | bytes 27456 | tf_op jit(solution)/shard_map/all_gather | solution.py:112
  128.9 0.6 cosine_reduce_fusion
  130.9 0.1 fusion.37
  131.0 0.5 multiply_bitcast_fusion
  131.5 19.7 %sine_negate_fusion = (f32[1440,721]{1,0:T(8,128)}, f32[1440,721]{1,0:T(8,128)}) fusion(), kind=kLoop, calls=%fused_computation.12 | loop fusion | flops 10382400 | bytes 8305920 | tf_op jit(solution)/shard_map/neg | solution.py:19
  151.2 4.8 %copy.28 = f32[4,360,1,416]{1,0,3,2:T(4,128)} copy(f32[4,360,1,416]{1,3,0,2:T(8,128)} %bitcast.7) | data formatting | bytes 4792320 | tf_op jit(solution)/shard_map/all_to_all | solution.py:83
  156.0 4.0 %squeeze.5 = f32[1440,416]{0,1:T(8,128)} reshape(f32[4,360,1,416]{1,0,3,2:T(4,128)} %copy.28) | data formatting | bytes 4792320 | tf_op jit(solution)/shard_map/squeeze | solution.py:83
  160.1 0.0 all-to-all-done
  160.1 3.1 %copy.25 = f32[4,360,1,416]{1,0,3,2:T(4,128)} copy(f32[4,360,1,416]{1,3,0,2:T(8,128)S(1)} %bitcast.42) | data formatting | bytes 4792320 | tf_op jit(solution)/shard_map/all_to_all | solution.py:82
  163.2 0.0 copy-start.1
  163.2 4.2 %squeeze.4 = f32[1440,416]{0,1:T(8,128)} reshape(f32[4,360,1,416]{1,0,3,2:T(4,128)} %copy.25) | data formatting | bytes 4792320 | tf_op jit(solution)/shard_map/squeeze | solution.py:82
  167.4 0.0 copy-done.1
  167.4 29.4 %fusion = f32[832,1442]{1,0:T(8,128)S(1)} fusion(f32[1440,721]{1,0:T(8,128)} %get-tuple-element.20, f32[1440,721]{1,0:T(8,128)} %get-tuple-element.21, f32[1440,416]{0,1:T(8,128)S(1)} %copy-done.1, f32[1440,416]{0,1:T(8,128)} %squeeze.4), kind=kOutput, calls=%fused_computation | convolution fusion | flops 20734851072 | bytes 17897216 | tf_op jit(solution)/shard_map/dot_general | solution.py:23
  196.8 0.4 slice_subtract_fusion
  197.2 0.7 fusion.25
  198.0 0.4 fusion.21
  198.4 2.1 pad_maximum_fusion
  200.5 5.6 %copy.29 = f32[416,3,721]{0,2,1:T(8,128)} copy(f32[416,3,721]{2,0,1:T(8,128)} %pad_maximum_fusion) | data formatting | bytes 7198464 | tf_op jit(solution)/shard_map/stack | solution.py:41
  206.1 4.9 %reshape.126 = f32[416,2163]{0,1:T(8,128)} reshape(f32[416,3,721]{0,2,1:T(8,128)} %copy.29) | data formatting | bytes 7198464 | tf_op jit(solution)/shard_map/reshape | solution.py:93
  210.9 5.2 %fusion.7 = f32[15,2163]{1,0:T(8,128)} fusion(f32[416,2163]{0,1:T(8,128)} %reshape.126, f32[416]{0:T(512)S(1)} %fusion.37, s32[416]{0:T(512)S(1)} %fusion.29), kind=kOutput, calls=%fused_computation.8 | convolution fusion | flops 162871488 | bytes 3732340 | tf_op jit(solution)/shard_map/dot_general | solution.py:100
  216.1 0.0 all-reduce.2.cloned.1.call-update
  216.2 62.5 %all-reduce.2.cloned.1.call-done = f32[15,2163]{1,0:T(8,128)} async-done(((f32[15,2163]{1,0:T(8,128)}), f32[15,2163]{1,0:T(8,128)}) %all-reduce.2.cloned.1.call-update) | async-done | bytes 129796 | tf_op jit(solution)/shard_map/psum | solution.py:103
  278.7 11.1 %all-gather.1 = f32[4,15,2163]{2,1,0:T(8,128)S(1)} all-gather(f32[1,15,2163]{2,1,0:T(8,128)} %bitcast.45), channel_id=1, replica_groups=mesh['lat'=8,'lon'=4] {'lon'}, dimensions={0}, use_global_device_ids=true | all-gather | bytes 648900 | tf_op jit(solution)/shard_map/all_gather | solution.py:104
  289.8 0.1 reshape.130
  289.8 0.4 fusion.26
  290.3 0.4 reshape.127
  290.7 0.9 copy.30
  (10 shorter events, 0.2 us)
Async XLA Ops:
  14.8 4.8 %copy-start = (f32[360,1664]{1,0:T(8,128)S(1)}, f32[360,1664]{1,0:T(8,128)}, u32[]{:S(2)}) copy-start(f32[360,1664]{1,0:T(8,128)} %param.3) | copy-start | bytes 7188484
  14.8 34.9 %all-to-all-start.1 = ((f32[360,4,416]{0,2,1:T(8,128)}), f32[360,4,416]{0,2,1:T(8,128)}, u32[]{:S(2)}, u32[]{:S(2)}) async-start(f32[360,4,416]{0,2,1:T(8,128)} %bitcast.43), calls=%async_computation.1 | async-start | bytes 5111808 | tf_op jit(solution)/shard_map/all_to_all | solution.py:83
  49.7 110.4 %all-to-all-start = ((f32[360,4,416]{0,2,1:T(8,128)}), f32[360,4,416]{0,2,1:T(8,128)S(1)}, u32[]{:S(2)}, u32[]{:S(2)}) async-start(f32[360,4,416]{0,2,1:T(8,128)} %bitcast.41), calls=%async_computation | async-start | bytes 5111808 | tf_op jit(solution)/shard_map/all_to_all | solution.py:82
  53.3 225.4 %all-reduce.2.cloned.1.call-start = ((), (), s32[]{:S(2)}) async-start(), calls=%async_computation.2 | async-start | bytes 278528 | tf_op jit(solution)/shard_map/psum | solution.py:103
  163.2 4.2 %copy-start.1 = (f32[1440,416]{0,1:T(8,128)S(1)}, f32[1440,416]{0,1:T(8,128)}, u32[]{:S(2)}) copy-start(f32[1440,416]{0,1:T(8,128)} %squeeze.5) | copy-start | bytes 7188484
Sparse Core Ops, SparseCore 0:
  216.3 62.3 all-reduce.1
